TPU v7x, 512 devices: a whole 4x4x16 slice. The times are simulated.
512 devices in a mesh: gx: 16 (over x, y_lo, core), gy: 32 (over y_hi, z).
Axes of the slice: x: 4, y: 4 (y_hi: 2, y_lo: 2; y = y_hi * 2 + y_lo), z: 16, core: 2. Of those that a mesh axis runs over, the one named last changes fastest.
Arguments:
- plate_motion: bfloat16 [32, 64, 128, 2, 128], P('gx', 'gy'), may hold values from -6 to 6
- adjoint_load: bfloat16 [32, 64, 128, 2, 128], P('gx', 'gy'), may hold values from -6 to 6
- excitation: bfloat16 [32, 64, 128, 2, 128], P('gx', 'gy'), may hold values from -6 to 6
- coupling: bfloat16 [32, 64, 5, 2, 128, 128], P('gx', 'gy'), may hold values from -0.25 to 0.25
- joints: int32 [32, 64, 4], P('gx', 'gy'), may hold values 0 or 1
- hydro: bfloat16 [2, 16384, 16384], P(None, 'gx', 'gy'), may hold values from -0.046875 to 0.046875
- panel_map: bfloat16 [16384, 2, 2, 128], P(('gx', 'gy')), may hold values from -0.25 to 0.25
Outputs:
- residual: float32 [32, 64, 128, 2, 128], P('gx', 'gy')
- multiplier: float32 [32, 64, 128, 2, 128], P('gx', 'gy')
- sensitivity: float32 [32, 64], P('gx', 'gy')
All inputs are finite; a program needn't handle non-finite values. No bound on the sum of `joints` on one device may be relied on, other than what follows from the above.
Results may differ from a plain program's by a relative error of at most 0.0031.
Values may be sent and summed in bfloat16 or wider, within the bound.
A program may use at most 64 MiB of HBM per device.

v0:
```python
import math
import jax
import jax.numpy as jnp
from jax import lax
from jax.sharding import PartitionSpec as P


def extended(x, sides, width):
    for axis, dim in sides:
        size, length = (lax.axis_size(axis), x.shape[dim])
        up = [(i, (i + 1) % size) for i in range(size - 1)]
        down = [(j, i) for i, j in up]
        last = lax.slice_in_dim(x, length - width, length, axis=dim)
        first = lax.slice_in_dim(x, 0, width, axis=dim)
        before = lax.ppermute(last, axis, up)
        after = lax.ppermute(first, axis, down)
        x = jnp.concatenate([before, x, after], axis=dim)
    return x


def complex_apply(form, coupling, vector):
    real_c = coupling[..., 0, :, :]
    imag_c = coupling[..., 1, :, :]
    real_v = vector[..., 0, :]
    imag_v = vector[..., 1, :]

    def mult(matrix, values):
        return jnp.einsum(form, matrix, values, preferred_element_type=jnp.float32)

    return jnp.stack(
        [mult(real_c, real_v) - mult(imag_c, imag_v), mult(real_c, imag_v) + mult(imag_c, real_v)],
        axis=-2,
    )


def adjoint_apply(form, coupling, vector):
    real_c = coupling[..., 0, :, :]
    imag_c = coupling[..., 1, :, :]
    real_v = vector[..., 0, :]
    imag_v = vector[..., 1, :]

    def mult(matrix, values):
        return jnp.einsum(form, matrix, values, preferred_element_type=jnp.float32)

    return jnp.stack(
        [mult(real_c, real_v) + mult(imag_c, imag_v), mult(real_c, imag_v) - mult(imag_c, real_v)],
        axis=-2,
    )


def plain_product(matrix, values):
    return jnp.dot(matrix, values, preferred_element_type=jnp.float32)


def flipped_product(matrix, values):
    return lax.dot_general(
        matrix, values, (((0,), (0,)), ((), ())), preferred_element_type=jnp.float32
    )


def on_device(plate_motion, adjoint_load, excitation, coupling, joints, hydro, panel_map):
    rows_count = plate_motion.shape[0]
    cols_count = plate_motion.shape[1]
    panel_count = panel_map.shape[0]
    unknowns = plate_motion.shape[4]
    cases = plate_motion.shape[2]
    links = joints.astype(jnp.float32)[:, :, :, None, None, None]
    padded = extended(plate_motion, (("gx", 0), ("gy", 1)), 1)
    beside_all = jnp.stack(
        [
            padded[0:rows_count, 1:-1],
            padded[2:, 1:-1],
            padded[1:-1, 0:cols_count],
            padded[1:-1, 2:],
        ],
        axis=2,
    )
    own = complex_apply("xyij,xyhj->xyhi", coupling[:, :, 0], plate_motion)
    structural = own + jnp.sum(
        links * complex_apply("xydij,xydhj->xydhi", coupling[:, :, 1:], beside_all), axis=2
    )
    outgoing = links * adjoint_apply("xydji,xyhj->xydhi", coupling[:, :, 1:], adjoint_load)
    own_adjoint = adjoint_apply("xyji,xyhj->xyhi", coupling[:, :, 0], adjoint_load)
    layered = extended(outgoing, (("gx", 0), ("gy", 1)), 1)
    incoming = (
        layered[2:, 1:-1, 0] + layered[:-2, 1:-1, 1] + layered[1:-1, 2:, 2] + layered[1:-1, :-2, 3]
    )
    lift = math.sqrt(rows_count * cols_count * unknowns / panel_count)
    motion_panels = jnp.einsum(
        "nxyk,xyhck->cnh", panel_map, plate_motion, preferred_element_type=jnp.float32
    ).astype(jnp.bfloat16)
    load_panels = jnp.einsum(
        "nxyk,xyhck->cnh", panel_map, adjoint_load, preferred_element_type=jnp.float32
    ).astype(jnp.bfloat16)
    piece = lax.all_gather(motion_panels, "gx", axis=1, tiled=True)
    first = plain_product(hydro[0], piece[0]) - plain_product(hydro[1], piece[1])
    second = plain_product(hydro[0], piece[1]) + plain_product(hydro[1], piece[0])
    pressure_part = jnp.stack([first, second])
    piece = lax.all_gather(load_panels, "gy", axis=1, tiled=True)
    first = flipped_product(hydro[0], piece[0]) + flipped_product(hydro[1], piece[1])
    second = flipped_product(hydro[0], piece[1]) - flipped_product(hydro[1], piece[0])
    reaction_part = jnp.stack([first, second])
    pressure_band = lax.psum(pressure_part, "gy")
    pressure = lax.dynamic_slice_in_dim(
        pressure_band, lax.axis_index("gy") * panel_count, panel_count, 1
    )
    reaction_band = lax.psum(reaction_part, "gx")
    reaction = lax.dynamic_slice_in_dim(
        reaction_band, lax.axis_index("gx") * panel_count, panel_count, 1
    )
    pressure = pressure.astype(jnp.bfloat16)
    reaction = reaction.astype(jnp.bfloat16)
    pressure_force = jnp.einsum(
        "nxyk,cnh->xyhck", panel_map, pressure, preferred_element_type=jnp.float32
    )
    reaction_force = jnp.einsum(
        "nxyk,cnh->xyhck", panel_map, reaction, preferred_element_type=jnp.float32
    )
    residual = structural + lift * pressure_force - excitation.astype(jnp.float32)
    multiplier = own_adjoint + incoming + lift * reaction_force
    sensitivity = jnp.sum(multiplier * own, axis=(2, 3, 4)) / math.sqrt(cases * unknowns)
    return (residual, multiplier, sensitivity)


def solution(mesh):
    placed = (
        P("gx", "gy", None, None, None),
        P("gx", "gy", None, None, None),
        P("gx", "gy", None, None, None),
        P("gx", "gy", None, None, None, None),
        P("gx", "gy", None),
        P(None, "gx", "gy"),
        P(("gx", "gy"), None, None, None),
    )
    return jax.shard_map(
        on_device,
        mesh=mesh,
        in_specs=placed,
        out_specs=(P("gx", "gy", None, None, None), P("gx", "gy", None, None, None), P("gx", "gy")),
        check_vma=False,
    )
```

profile of v0, /device:TPU:14, one launch (start us, length us, event | category | flops | bytes accessed | tf_op | source)
XLA Modules:
  0.0 440.0 jit_solution(6919222201309677431)
XLA Ops:
  0.6 1.0 copy.43
  1.7 0.7 fusion.106
  2.4 1.9 collective-permute-start
  4.3 3.6 collective-permute-start.1
  8.0 1.3 slice_bitcast_fusion.2
  9.4 1.3 fusion.59
  10.9 1.0 copy_bitcast_fusion
  12.1 84.5 %all_gather.7 = bf16[2,1024,128]{2,1,0:T(8,128)(2,1)S(1)} all-gather(bf16[2,32,128]{2,1,0:T(8,128)(2,1)S(1)} %fusion.19), channel_id=1, replica_groups=mesh['gx'=16,'gy'=32] {'gy'}, dimensions={1}, use_global_device_ids=true | all-gather | bytes 540672 | tf_op jit(solution)/shard_map/all_gather | solution.py:99
  96.6 1.2 fusion.25
  97.9 1.2 fusion.27
  99.3 16.8 %all_gather.6 = bf16[2,512,128]{2,1,0:T(8,128)(2,1)S(1)} all-gather(bf16[2,32,128]{2,1,0:T(8,128)(2,1)S(1)} %fusion.20), channel_id=1, replica_groups=mesh['gx'=16,'gy'=32] {'gx'}, dimensions={1}, use_global_device_ids=true | all-gather | bytes 278528 | tf_op jit(solution)/shard_map/all_gather | solution.py:95
  116.2 1.2 fusion.29
  117.4 1.2 fusion.31
  118.9 2.0 fusion.15
  120.9 1.6 fusion.16
  122.6 0.4 fusion.5
  123.0 0.4 fusion.6
  123.5 0.3 copy-done
  124.4 0.6 copy-done.5
  125.1 0.9 constant_dynamic-update-slice_fusion
  126.1 1.3 collective-permute-start.2
  127.4 1.3 collective-permute-start.3
  128.7 1.1 pad_maximum_fusion.2
  129.9 0.9 fusion.66
  130.8 2.9 collective-permute-done.2
  133.7 4.1 collective-permute-done.3
  138.1 0.5 fusion.51
  138.6 0.5 fusion.47
  139.1 0.5 fusion.4
  139.6 0.5 fusion.3
  140.1 1.3 maximum_multiply_fusion.1
  141.3 1.6 fusion.104
  142.9 1.9 collective-permute-start.4
  144.8 3.4 collective-permute-start.5
  148.2 0.8 pad_maximum_fusion.12
  149.4 0.9 fusion.12
  150.7 18.0 %collective-permute-done.4 = f32[1,2,4,128,2,128]{5,3,1,0,4,2:T(8,128)} collective-permute-done((f32[1,2,4,128,2,128]{5,3,1,0,4,2:T(8,128)}, f32[1,2,4,128,2,128]{5,3,1,0,4,2:T(8,128)}, u32[]{:S(2)}, u32[]{:S(2)}) %collective-permute-start.4) | collective-permute-done | bytes 1048608 | tf_op jit(solution)/shard_map/ppermute | solution.py:16
  168.7 2.0 pad_maximum_fusion
  170.7 2.5 fusion.103
  173.2 1.4 collective-permute-start.6
  174.6 5.9 %collective-permute-start.7 = (f32[4,1,4,128,2,128]{5,3,1,0,4,2:T(8,128)}, f32[4,1,4,128,2,128]{5,3,1,0,4,2:T(8,128)}, u32[]{:S(2)}, u32[]{:S(2)}) collective-permute-start(f32[4,1,4,128,2,128]{5,3,1,0,4,2:T(8,128)} %get-tuple-element.10), channel_id=1, source_target_pairs={{0,1},{1,2},{2,3},{3,4},{4,5},{5,6},{6,7},{7,8},{8,9},{9,10},{10,1... | collective-permute-start | bytes 6291464 | tf_op jit(solution)/shard_map/ppermute | solution.py:15
  181.0 98.1 %all-reduce.2 = bf16[2,512,128]{2,1,0:T(8,128)(2,1)} all-reduce(f32[2,512,128]{2,1,0:T(8,128)} %pad_maximum_fusion.12), channel_id=1, replica_groups=mesh['gx'=16,'gy'=32] {'gx'}, use_global_device_ids=true, to_apply=%region_2.0 | all-reduce | flops 131072 | bytes 786432 | tf_op jit(solution)/shard_map/psum | solution.py:107
  279.1 154.9 %all-reduce.3 = bf16[2,1024,128]{2,1,0:T(8,128)(2,1)} all-reduce(f32[2,1024,128]{2,1,0:T(8,128)} %pad_maximum_fusion.2), channel_id=1, replica_groups=mesh['gx'=16,'gy'=32] {'gy'}, use_global_device_ids=true, to_apply=%region_1.0 | all-reduce | flops 262144 | bytes 1572864 | tf_op jit(solution)/shard_map/psum | solution.py:103
  434.0 1.4 fusion.10
  435.4 1.2 copy.80
  436.6 1.6 multiply_reduce_fusion
  438.2 1.2 copy.81
  439.4 0.6 broadcast_multiply_fusion
  (50 shorter events, 3.1 us)
Async XLA Ops:
  0.6 8.6 %copy-start.9 = (bf16[2,2,128,2,128]{4,3,2,1,0:T(2,128)(2,1)S(1)}, bf16[2,2,128,2,128]{4,3,2,1,0:T(2,128)(2,1)}, u32[]{:S(2)}) copy-start(bf16[2,2,128,2,128]{4,3,2,1,0:T(2,128)(2,1)} %param.8) | copy-start | bytes 786436
  2.4 122.0 %collective-permute-start = (bf16[1,2,128,2,128]{4,2,1,0,3:T(8,128)(2,1)}, bf16[1,2,128,2,128]{4,2,1,0,3:T(8,128)(2,1)S(1)}, u32[]{:S(2)}, u32[]{:S(2)}) collective-permute-start(bf16[1,2,128,2,128]{4,2,1,0,3:T(8,128)(2,1)} %get-tuple-element.24), channel_id=1, source_target_pairs={{0,32},{32,64},{64,96},{96,128},{128,160},{160,192},{192,224},{224... | collective-permute-start | bytes 393224 | tf_op jit(solution)/shard_map/ppermute | solution.py:15
  4.3 120.8 %collective-permute-start.1 = (bf16[1,2,128,2,128]{4,2,1,0,3:T(8,128)(2,1)}, bf16[1,2,128,2,128]{4,2,1,0,3:T(8,128)(2,1)}, u32[]{:S(2)}, u32[]{:S(2)}) collective-permute-start(bf16[1,2,128,2,128]{4,2,1,0,3:T(8,128)(2,1)} %get-tuple-element.23), channel_id=1, source_target_pairs={{32,0},{64,32},{96,64},{128,96},{160,128},{192,160},{224,192},{256... | collective-permute-start | bytes 393224 | tf_op jit(solution)/shard_map/ppermute | solution.py:16
  9.3 2.6 copy-start.10
  9.3 87.3 %copy-start.1 = (bf16[2,1024,512]{2,1,0:T(8,128)(2,1)S(1)}, bf16[2,1024,512]{2,1,0:T(8,128)(2,1)}, u32[]{:S(2)}) copy-start(bf16[2,1024,512]{2,1,0:T(8,128)(2,1)} %param.12) | copy-start | bytes 6291460
  12.1 87.0 %copy-start.4 = (bf16[2,2,128,2,128]{4,3,2,1,0:T(2,128)(2,1)S(1)}, bf16[2,2,128,2,128]{4,3,2,1,0:T(2,128)(2,1)}, u32[]{:S(2)}) copy-start(bf16[2,2,128,2,128]{4,3,2,1,0:T(2,128)(2,1)} %param.7) | copy-start | bytes 786436
  96.6 19.5 %copy-start.8 = (bf16[2,1024,128]{2,1,0:T(8,128)(2,1)}, bf16[2,1024,128]{2,1,0:T(8,128)(2,1)S(1)}, u32[]{:S(2)}) copy-start(bf16[2,1024,128]{2,1,0:T(8,128)(2,1)S(1)} %all_gather.7) | copy-start | bytes 1572868
  99.1 19.5 %copy-start.12 = (s32[2,2,4]{2,1,0:T(2,128)S(1)}, s32[2,2,4]{2,1,0:T(2,128)}, u32[]{:S(2)}) copy-start(s32[2,2,4]{2,1,0:T(2,128)} %param.11) | copy-start | bytes 196
  118.7 2.2 copy-start.2
  118.7 3.8 copy-start.7
  120.9 2.1 copy-start.6
  122.6 1.2 copy-start
  124.1 1.0 copy-start.5
  126.1 7.6 %collective-permute-start.2 = (bf16[4,1,128,2,128]{4,2,1,0,3:T(8,128)(2,1)S(1)}, bf16[4,1,128,2,128]{4,2,1,0,3:T(8,128)(2,1)S(1)}, u32[]{:S(2)}, u32[]{:S(2)}) collective-permute-start(bf16[4,1,128,2,128]{4,2,1,0,3:T(8,128)(2,1)S(1)} %get-tuple-element.19), channel_id=1, source_target_pairs={{0,1},{1,2},{2,3},{3,4},{4,5},{5,6},{6,7},{7,8},{8,9},{9,10},{10,1... | collective-permute-start | bytes 786440 | tf_op jit(solution)/shard_map/ppermute | solution.py:15
  127.4 10.4 %collective-permute-start.3 = (bf16[4,1,128,2,128]{4,2,1,0,3:T(8,128)(2,1)S(1)}, bf16[4,1,128,2,128]{4,2,1,0,3:T(8,128)(2,1)S(1)}, u32[]{:S(2)}, u32[]{:S(2)}) collective-permute-start(bf16[4,1,128,2,128]{4,2,1,0,3:T(8,128)(2,1)S(1)} %get-tuple-element.20), channel_id=1, source_target_pairs={{1,0},{2,1},{3,2},{4,3},{5,4},{6,5},{7,6},{8,7},{9,8},{10,9},{11,1... | collective-permute-start | bytes 786440 | tf_op jit(solution)/shard_map/ppermute | solution.py:16
  142.9 25.8 %collective-permute-start.4 = (f32[1,2,4,128,2,128]{5,3,1,0,4,2:T(8,128)}, f32[1,2,4,128,2,128]{5,3,1,0,4,2:T(8,128)}, u32[]{:S(2)}, u32[]{:S(2)}) collective-permute-start(f32[1,2,4,128,2,128]{5,3,1,0,4,2:T(8,128)} %get-tuple-element.12), channel_id=1, source_target_pairs={{32,0},{64,32},{96,64},{128,96},{160,128},{192,160},{224,192},{256... | collective-permute-start | bytes 3145736 | tf_op jit(solution)/shard_map/ppermute | solution.py:16
  144.8 23.8 %collective-permute-start.5 = (f32[1,2,4,128,2,128]{5,3,1,0,4,2:T(8,128)}, f32[1,2,4,128,2,128]{5,3,1,0,4,2:T(8,128)}, u32[]{:S(2)}, u32[]{:S(2)}) collective-permute-start(f32[1,2,4,128,2,128]{5,3,1,0,4,2:T(8,128)} %get-tuple-element.11), channel_id=1, source_target_pairs={{0,32},{32,64},{64,96},{96,128},{128,160},{160,192},{192,224},{224... | collective-permute-start | bytes 3145736 | tf_op jit(solution)/shard_map/ppermute | solution.py:15
  173.2 260.8 %copy-start.11 = (bf16[32,2,2,128]{3,2,1,0:T(2,128)(2,1)S(1)}, bf16[32,2,2,128]{3,2,1,0:T(2,128)(2,1)}, u32[]{:S(2)}) copy-start(bf16[32,2,2,128]{3,2,1,0:T(2,128)(2,1)} %param.13) | copy-start | bytes 98308
  173.2 263.4 %collective-permute-start.6 = (f32[4,1,4,128,2,128]{5,3,1,0,4,2:T(8,128)}, f32[4,1,4,128,2,128]{5,3,1,0,4,2:T(8,128)}, u32[]{:S(2)}, u32[]{:S(2)}) collective-permute-start(f32[4,1,4,128,2,128]{5,3,1,0,4,2:T(8,128)} %get-tuple-element.9), channel_id=1, source_target_pairs={{1,0},{2,1},{3,2},{4,3},{5,4},{6,5},{7,6},{8,7},{9,8},{10,9},{11,1... | collective-permute-start | bytes 6291464 | tf_op jit(solution)/shard_map/ppermute | solution.py:16
  174.6 262.0 %collective-permute-start.7 = (f32[4,1,4,128,2,128]{5,3,1,0,4,2:T(8,128)}, f32[4,1,4,128,2,128]{5,3,1,0,4,2:T(8,128)}, u32[]{:S(2)}, u32[]{:S(2)}) collective-permute-start(f32[4,1,4,128,2,128]{5,3,1,0,4,2:T(8,128)} %get-tuple-element.10), channel_id=1, source_target_pairs={{0,1},{1,2},{2,3},{3,4},{4,5},{5,6},{6,7},{7,8},{8,9},{9,10},{10,1... | collective-permute-start | bytes 6291464 | tf_op jit(solution)/shard_map/ppermute | solution.py:15
  434.0 2.7 copy-start.3
where the time goes:
time: 441 us; the launch traced here: 440 us
  blocking collectives  354 us (80%)
  waiting for transfers between devices  25.1 us (6%)
  starting transfers between devices  20.7 us (5%)
  matrix products  19 us (4%)
  local copies, waits for them, and re-layouts  12.8 us (3%)
  other arithmetic  6.95 us (2%)
    psum x1, blocking collectives, on_device(): pressure_band = lax.psum(pressure_part, 'gy')  155 us
    psum x1, blocking collectives, on_device(): reaction_band = lax.psum(reaction_part, 'gx')  98.1 us
    all_gather x1, blocking collectives, on_device(): piece = lax.all_gather(load_panels, 'gy', axis=1, tiled=True)  84.5 us
    ppermute x4, waiting for transfers between devices, extended(): after = lax.ppermute(first, axis, down)  22.1 us
    all_gather x1, blocking collectives, on_device(): piece = lax.all_gather(motion_panels, 'gx', axis=1, tiled=True)  16.8 us
    ppermute x4, starting transfers between devices, extended(): before = lax.ppermute(last, axis, up)  12.5 us
  transfers between devices with their start and end apart: 8, of which 3 were waited for; matrix products, arithmetic and copies ran while one was open for 5% of the time, Pallas kernels for 0%

commit v1 on v0

--- a/solution.py
+++ b/solution.py
@@ -96,7 +96,9 @@
     first = plain_product(hydro[0], piece[0]) - plain_product(hydro[1], piece[1])
     second = plain_product(hydro[0], piece[1]) + plain_product(hydro[1], piece[0])
     pressure_part = jnp.stack([first, second])
-    piece = lax.all_gather(load_panels, "gy", axis=1, tiled=True)
+    piece = jnp.concatenate(
+        lax.all_to_all(jnp.stack([load_panels] * lax.axis_size("gy")), "gy", 0, 0), axis=1
+    )
     first = flipped_product(hydro[0], piece[0]) + flipped_product(hydro[1], piece[1])
     second = flipped_product(hydro[0], piece[1]) - flipped_product(hydro[1], piece[0])
     reaction_part = jnp.stack([first, second])

time: 441 us -> 338 us (0.77)
  the two profiles are of different devices: /device:TPU:14 before, /device:TPU:1 now
where the time goes in v1:
time: 338 us
  blocking collectives  251 us (74%)
  starting transfers between devices  41 us (12%)
  matrix products  17.2 us (5%)
  local copies, waits for them, and re-layouts  14.3 us (4%)
  other arithmetic  7.74 us (2%)
  waiting for transfers between devices  5.52 us (2%)
    psum x1, blocking collectives, on_device(): pressure_band = lax.psum(pressure_part, 'gy')  132 us
    psum x1, blocking collectives, on_device(): reaction_band = lax.psum(reaction_part, 'gx')  97.7 us
    all_gather x1, blocking collectives, on_device(): piece = lax.all_gather(motion_panels, 'gx', axis=1, tiled=True)  20.6 us
    ppermute x4, starting transfers between devices, extended(): before = lax.ppermute(last, axis, up)  15.6 us
    all_to_all x1, starting transfers between devices, on_device(): lax.all_to_all(jnp.stack([load_panels] * lax.axis_size('gy')), 'gy', 0, 0)  14.1 us
    ppermute x4, starting transfers between devices, extended(): after = lax.ppermute(first, axis, down)  11.3 us
    dot_general x16, matrix products, mult(): return jnp.einsum(form, matrix, values, preferred_element_type=jnp.float32)  7.89 us
  transfers between devices with their start and end apart: 9, of which 2 were waited for; matrix products, arithmetic and copies ran while one was open for 10% of the time, Pallas kernels for 0%

profile of v1, /device:TPU:1, one launch (start us, length us, event | category | flops | bytes accessed | tf_op | source)
XLA Modules:
  0.0 337.7 jit_solution(4934027351917285798)
XLA Ops:
  0.7 1.1 copy.43
  1.8 0.7 fusion.107
  2.5 4.6 %collective-permute-start = (bf16[1,2,128,2,128]{4,2,1,0,3:T(8,128)(2,1)}, bf16[1,2,128,2,128]{4,2,1,0,3:T(8,128)(2,1)S(1)}, u32[]{:S(2)}, u32[]{:S(2)}) collective-permute-start(bf16[1,2,128,2,128]{4,2,1,0,3:T(8,128)(2,1)} %get-tuple-element.26), channel_id=1, source_target_pairs={{0,32},{32,64},{64,96},{96,128},{128,160},{160,192},{192,224},{224... | collective-permute-start | bytes 393224 | tf_op jit(solution)/shard_map/ppermute | solution.py:15
  7.1 5.5 %collective-permute-start.1 = (bf16[1,2,128,2,128]{4,2,1,0,3:T(8,128)(2,1)}, bf16[1,2,128,2,128]{4,2,1,0,3:T(8,128)(2,1)}, u32[]{:S(2)}, u32[]{:S(2)}) collective-permute-start(bf16[1,2,128,2,128]{4,2,1,0,3:T(8,128)(2,1)} %get-tuple-element.25), channel_id=1, source_target_pairs={{32,0},{64,32},{96,64},{128,96},{160,128},{192,160},{224,192},{256... | collective-permute-start | bytes 393224 | tf_op jit(solution)/shard_map/ppermute | solution.py:16
  12.6 1.1 fusion.19
  13.7 0.9 stack.124
  14.6 14.1 %all-to-all-start = ((bf16[32,2,32,128]{3,2,1,0:T(8,128)(2,1)}), bf16[32,2,32,128]{3,2,1,0:T(8,128)(2,1)}, u32[]{:S(2)}, u32[]{:S(2)}) async-start(bf16[32,2,32,128]{3,2,1,0:T(8,128)(2,1)} %stack.124), calls=%async_computation | async-start | bytes 1048576 | tf_op jit(solution)/shard_map/all_to_all | solution.py:100
  30.1 0.9 fusion.77
  31.2 20.6 %all_gather.3 = bf16[2,512,128]{2,1,0:T(8,128)(2,1)S(1)} all-gather(bf16[2,32,128]{2,1,0:T(8,128)(2,1)S(1)} %fusion.20), channel_id=1, replica_groups=mesh['gx'=16,'gy'=32] {'gx'}, dimensions={1}, use_global_device_ids=true | all-gather | bytes 278528 | tf_op jit(solution)/shard_map/all_gather | solution.py:95
  52.7 1.3 fusion.2
  53.9 1.3 fusion.1
  56.1 1.1 pad_maximum_fusion.2
  57.4 0.9 constant_dynamic-update-slice_fusion
  58.4 0.8 fusion.106
  59.2 3.4 collective-permute-start.2
  62.5 1.3 collective-permute-start.3
  63.8 0.9 fusion.12
  65.0 1.0 fusion.66
  66.0 2.4 collective-permute-done.2
  68.4 0.7 copy-done.9
  69.1 3.1 collective-permute-done.3
  72.2 1.0 fusion.64
  73.5 0.5 fusion.51
  73.9 0.5 fusion.47
  74.4 0.5 fusion.4
  74.9 0.5 fusion.3
  75.4 0.7 copy-done.2
  76.5 1.3 maximum_multiply_fusion.1
  77.7 1.4 fusion.104
  79.2 3.2 collective-permute-start.4
  82.4 2.4 collective-permute-start.5
  84.7 132.5 %all-reduce.3 = bf16[2,1024,128]{2,1,0:T(8,128)(2,1)} all-reduce(f32[2,1024,128]{2,1,0:T(8,128)} %pad_maximum_fusion.2), channel_id=1, replica_groups=mesh['gx'=16,'gy'=32] {'gy'}, use_global_device_ids=true, to_apply=%region_1.0 | all-reduce | flops 262144 | bytes 1572864 | tf_op jit(solution)/shard_map/psum | solution.py:105
  217.3 1.9 pad_maximum_fusion
  219.2 2.5 fusion.103
  221.7 1.3 collective-permute-start.6
  223.0 5.3 %collective-permute-start.7 = (f32[4,1,4,128,2,128]{5,3,1,0,4,2:T(8,128)}, f32[4,1,4,128,2,128]{5,3,1,0,4,2:T(8,128)}, u32[]{:S(2)}, u32[]{:S(2)}) collective-permute-start(f32[4,1,4,128,2,128]{5,3,1,0,4,2:T(8,128)} %get-tuple-element.10), channel_id=1, source_target_pairs={{0,1},{1,2},{2,3},{3,4},{4,5},{5,6},{6,7},{7,8},{8,9},{9,10},{10,1... | collective-permute-start | bytes 6291464 | tf_op jit(solution)/shard_map/ppermute | solution.py:15
  228.5 1.4 fusion.10
  229.9 1.2 copy.80
  231.1 1.2 fusion.105
  232.4 1.8 fusion.25
  234.1 0.5 fusion.15
  234.7 0.5 fusion.27
  235.2 0.5 fusion.16
  235.7 0.8 pad_maximum_fusion.12
  236.6 97.7 %all-reduce.2 = bf16[2,512,128]{2,1,0:T(8,128)(2,1)S(1)} all-reduce(f32[2,512,128]{2,1,0:T(8,128)} %pad_maximum_fusion.12), channel_id=1, replica_groups=mesh['gx'=16,'gy'=32] {'gx'}, use_global_device_ids=true, to_apply=%region_2.0 | all-reduce | flops 131072 | bytes 786432 | tf_op jit(solution)/shard_map/psum | solution.py:109
  334.3 1.6 multiply_reduce_fusion
  335.9 1.2 copy.81
  337.1 0.6 broadcast_multiply_fusion
  (53 shorter events, 4.5 us)
Async XLA Ops:
  0.6 28.1 %copy-start.8 = (bf16[2,2,128,2,128]{4,3,2,1,0:T(2,128)(2,1)S(1)}, bf16[2,2,128,2,128]{4,3,2,1,0:T(2,128)(2,1)}, u32[]{:S(2)}) copy-start(bf16[2,2,128,2,128]{4,3,2,1,0:T(2,128)(2,1)} %param.8) | copy-start | bytes 786436
  0.6 28.2 %copy-start.4 = (bf16[2,2,5,2,128,128]{5,4,3,2,1,0:T(8,128)(2,1)S(1)}, bf16[2,2,5,2,128,128]{5,4,3,2,1,0:T(8,128)(2,1)}, u32[]{:S(2)}) copy-start(bf16[2,2,5,2,128,128]{5,4,3,2,1,0:T(8,128)(2,1)} %param.10) | copy-start | bytes 3932164
  2.5 54.8 %collective-permute-start = (bf16[1,2,128,2,128]{4,2,1,0,3:T(8,128)(2,1)}, bf16[1,2,128,2,128]{4,2,1,0,3:T(8,128)(2,1)S(1)}, u32[]{:S(2)}, u32[]{:S(2)}) collective-permute-start(bf16[1,2,128,2,128]{4,2,1,0,3:T(8,128)(2,1)} %get-tuple-element.26), channel_id=1, source_target_pairs={{0,32},{32,64},{64,96},{96,128},{128,160},{160,192},{192,224},{224... | collective-permute-start | bytes 393224 | tf_op jit(solution)/shard_map/ppermute | solution.py:15
  7.1 50.4 %collective-permute-start.1 = (bf16[1,2,128,2,128]{4,2,1,0,3:T(8,128)(2,1)}, bf16[1,2,128,2,128]{4,2,1,0,3:T(8,128)(2,1)}, u32[]{:S(2)}, u32[]{:S(2)}) collective-permute-start(bf16[1,2,128,2,128]{4,2,1,0,3:T(8,128)(2,1)} %get-tuple-element.25), channel_id=1, source_target_pairs={{32,0},{64,32},{96,64},{128,96},{160,128},{192,160},{224,192},{256... | collective-permute-start | bytes 393224 | tf_op jit(solution)/shard_map/ppermute | solution.py:16
  14.6 216.5 %all-to-all-start = ((bf16[32,2,32,128]{3,2,1,0:T(8,128)(2,1)}), bf16[32,2,32,128]{3,2,1,0:T(8,128)(2,1)}, u32[]{:S(2)}, u32[]{:S(2)}) async-start(bf16[32,2,32,128]{3,2,1,0:T(8,128)(2,1)} %stack.124), calls=%async_computation | async-start | bytes 1048576 | tf_op jit(solution)/shard_map/all_to_all | solution.py:100
  29.2 1.8 copy-start.7
  29.2 1.8 copy-start.10
  29.2 22.6 %copy-start = (bf16[2,1024,512]{2,1,0:T(8,128)(2,1)S(1)}, bf16[2,1024,512]{2,1,0:T(8,128)(2,1)}, u32[]{:S(2)}) copy-start(bf16[2,1024,512]{2,1,0:T(8,128)(2,1)} %param.12) | copy-start | bytes 6291460
  57.1 7.6 %copy-start.12 = (s32[2,2,4]{2,1,0:T(2,128)S(1)}, s32[2,2,4]{2,1,0:T(2,128)}, u32[]{:S(2)}) copy-start(s32[2,2,4]{2,1,0:T(2,128)} %param.11) | copy-start | bytes 196
  59.2 9.2 %collective-permute-start.2 = (bf16[4,1,128,2,128]{4,2,1,0,3:T(8,128)(2,1)}, bf16[4,1,128,2,128]{4,2,1,0,3:T(8,128)(2,1)S(1)}, u32[]{:S(2)}, u32[]{:S(2)}) collective-permute-start(bf16[4,1,128,2,128]{4,2,1,0,3:T(8,128)(2,1)} %get-tuple-element.21), channel_id=1, source_target_pairs={{0,1},{1,2},{2,3},{3,4},{4,5},{5,6},{6,7},{7,8},{8,9},{9,10},{10,1... | collective-permute-start | bytes 786440 | tf_op jit(solution)/shard_map/ppermute | solution.py:15
  62.5 9.7 %collective-permute-start.3 = (bf16[4,1,128,2,128]{4,2,1,0,3:T(8,128)(2,1)}, bf16[4,1,128,2,128]{4,2,1,0,3:T(8,128)(2,1)}, u32[]{:S(2)}, u32[]{:S(2)}) collective-permute-start(bf16[4,1,128,2,128]{4,2,1,0,3:T(8,128)(2,1)} %get-tuple-element.22), channel_id=1, source_target_pairs={{1,0},{2,1},{3,2},{4,3},{5,4},{6,5},{7,6},{8,7},{9,8},{10,9},{11,1... | collective-permute-start | bytes 786440 | tf_op jit(solution)/shard_map/ppermute | solution.py:16
  68.4 0.7 copy-start.9
  74.9 1.2 copy-start.2
  74.9 1.5 copy-start.3
  79.2 138.1 %collective-permute-start.4 = (f32[1,2,4,128,2,128]{5,3,1,0,4,2:T(8,128)}, f32[1,2,4,128,2,128]{5,3,1,0,4,2:T(8,128)}, u32[]{:S(2)}, u32[]{:S(2)}) collective-permute-start(f32[1,2,4,128,2,128]{5,3,1,0,4,2:T(8,128)} %get-tuple-element.12), channel_id=1, source_target_pairs={{32,0},{64,32},{96,64},{128,96},{160,128},{192,160},{224,192},{256... | collective-permute-start | bytes 3145736 | tf_op jit(solution)/shard_map/ppermute | solution.py:16
  82.4 134.9 %collective-permute-start.5 = (f32[1,2,4,128,2,128]{5,3,1,0,4,2:T(8,128)}, f32[1,2,4,128,2,128]{5,3,1,0,4,2:T(8,128)}, u32[]{:S(2)}, u32[]{:S(2)}) collective-permute-start(f32[1,2,4,128,2,128]{5,3,1,0,4,2:T(8,128)} %get-tuple-element.11), channel_id=1, source_target_pairs={{0,32},{32,64},{64,96},{96,128},{128,160},{160,192},{192,224},{224... | collective-permute-start | bytes 3145736 | tf_op jit(solution)/shard_map/ppermute | solution.py:15
  219.2 9.1 %copy-start.6 = (f32[2,2,128,128]{3,2,1,0:T(8,128)S(1)}, f32[2,2,128,128]{3,2,1,0:T(8,128)}, u32[]{:S(2)}) copy-start(f32[2,2,128,128]{3,2,1,0:T(8,128)} %fusion.77) | copy-start | bytes 786436
  219.2 9.4 %copy-start.11 = (bf16[32,2,2,128]{3,2,1,0:T(2,128)(2,1)S(1)}, bf16[32,2,2,128]{3,2,1,0:T(2,128)(2,1)}, u32[]{:S(2)}) copy-start(bf16[32,2,2,128]{3,2,1,0:T(2,128)(2,1)} %param.13) | copy-start | bytes 98308
  221.7 112.6 %collective-permute-start.6 = (f32[4,1,4,128,2,128]{5,3,1,0,4,2:T(8,128)}, f32[4,1,4,128,2,128]{5,3,1,0,4,2:T(8,128)}, u32[]{:S(2)}, u32[]{:S(2)}) collective-permute-start(f32[4,1,4,128,2,128]{5,3,1,0,4,2:T(8,128)} %get-tuple-element.9), channel_id=1, source_target_pairs={{1,0},{2,1},{3,2},{4,3},{5,4},{6,5},{7,6},{8,7},{9,8},{10,9},{11,1... | collective-permute-start | bytes 6291464 | tf_op jit(solution)/shard_map/ppermute | solution.py:16
  223.0 111.3 %collective-permute-start.7 = (f32[4,1,4,128,2,128]{5,3,1,0,4,2:T(8,128)}, f32[4,1,4,128,2,128]{5,3,1,0,4,2:T(8,128)}, u32[]{:S(2)}, u32[]{:S(2)}) collective-permute-start(f32[4,1,4,128,2,128]{5,3,1,0,4,2:T(8,128)} %get-tuple-element.10), channel_id=1, source_target_pairs={{0,1},{1,2},{2,3},{3,4},{4,5},{5,6},{6,7},{7,8},{8,9},{9,10},{10,1... | collective-permute-start | bytes 6291464 | tf_op jit(solution)/shard_map/ppermute | solution.py:15
  231.1 3.0 copy-start.1
  235.2 99.1 %copy-start.5 = (f32[2,2,128,1,128]{4,2,1,0,3:T(8,128)S(1)}, f32[2,2,128,1,128]{4,2,1,0,3:T(8,128)}, u32[]{:S(2)}) copy-start(f32[2,2,128,1,128]{4,2,1,0,3:T(8,128)} %fusion.12) | copy-start | bytes 786436
